TPU v7x, 128 devices: a whole 4x4x4 slice. The times are simulated.
128 devices in a mesh: expert: 32 (over z, x, core), replica: 4 (over y).
Axes of the slice: x: 4, y: 4, z: 4, core: 2. Of those that a mesh axis runs over, the one named last changes fastest.
Arguments:
- x_tokens: bfloat16 [16384, 2048], P(('expert', 'replica')), may hold values from -6 to 6
- d_out: bfloat16 [16384, 2048], P(('expert', 'replica')), may hold values from -3 to 3
- expert_ids: int32 [16384, 2], P(('expert', 'replica')), may hold values from 0 to 31, all different within a row; in each aligned block of 128 rows (0 to 127, 128 to 255, ...) at most 16 rows name the same one
- combine: float32 [16384, 2], P(('expert', 'replica')), may hold values from 0.1 to 1
- w_stack: bfloat16 [32, 1408, 6144], P('expert'), may hold values from -0.125 to 0.125
Outputs:
- d_tokens: bfloat16 [16384, 2048], P(('expert', 'replica'))
- g_stack: bfloat16 [32, 1408, 6144], P('expert', 'replica')
Inputs may be any that keep to these rules, and one draw needn't show every extreme that they name: `expert_ids`: in the tokens of one device (aligned blocks of 128 tokens) each expert is named by at most 16 routes, and by exactly 16 in some block; a token's 2 experts differ.
All inputs are finite; a program needn't handle non-finite values.
Results may differ from a plain program's by a relative error of at most 0.013.
Values may be sent and summed in bfloat16 or wider, within the bound.
A program may use at most 128 MiB of HBM per device.

v0:
```python
import jax
import jax.numpy as jnp
from jax import lax
from jax.sharding import PartitionSpec as P


def contract_rows(factor, operand):
    return lax.dot_general(
        factor, operand, (((0,), (0,)), ((), ())), preferred_element_type=jnp.float32
    )


def body(x_tokens, d_out, expert_ids, combine, w_stack):
    tok_count, feat_width = x_tokens.shape
    top_count = expert_ids.shape[1]
    expert_count = lax.axis_size("expert")
    capacity = 2 * tok_count * top_count // expert_count
    route_count = tok_count * top_count
    slot_total = expert_count * capacity
    weights = w_stack[0]
    hidden = weights.shape[0]
    w_gate = weights[:, :feat_width]
    w_up = weights[:, feat_width : 2 * feat_width]
    w_down = weights[:, 2 * feat_width :]
    flat_ids = expert_ids.reshape(route_count)
    member = (flat_ids[:, None] == jnp.arange(expert_count, dtype=jnp.int32)[None, :]).astype(
        jnp.int32
    )
    slot_rank = jnp.sum((jnp.cumsum(member, axis=0) - 1) * member, axis=1)
    slot_index = flat_ids * capacity + slot_rank
    placing = (jnp.arange(slot_total, dtype=jnp.int32)[:, None] == slot_index[None, :]).astype(
        jnp.bfloat16
    )
    x_routes = jnp.repeat(x_tokens, top_count, axis=0)
    dy_routes = (
        combine.reshape(route_count, 1) * jnp.repeat(d_out, top_count, axis=0).astype(jnp.float32)
    ).astype(jnp.bfloat16)
    send_x = jnp.dot(placing, x_routes, preferred_element_type=jnp.float32).astype(jnp.bfloat16)
    send_x = send_x.reshape(expert_count, capacity, feat_width)
    send_dy = jnp.dot(placing, dy_routes, preferred_element_type=jnp.float32).astype(jnp.bfloat16)
    send_dy = send_dy.reshape(expert_count, capacity, feat_width)
    x_slots = lax.all_to_all(send_x, "expert", split_axis=0, concat_axis=0, tiled=True)
    dy_slots = lax.all_to_all(send_dy, "expert", split_axis=0, concat_axis=0, tiled=True)
    lead_count, item_count, _ = x_slots.shape
    row_block = x_slots.reshape(lead_count * item_count, feat_width)
    grads_in = dy_slots.reshape(lead_count * item_count, feat_width)
    last_dims = (((1,), (1,)), ((), ()))
    gate_pre = lax.dot_general(row_block, w_gate, last_dims, preferred_element_type=jnp.float32)
    up_pre = lax.dot_general(row_block, w_up, last_dims, preferred_element_type=jnp.float32)
    d_hidden = lax.dot_general(grads_in, w_down, last_dims, preferred_element_type=jnp.float32)
    gate_sigmoid = jax.nn.sigmoid(gate_pre)
    gate_act = gate_pre * gate_sigmoid
    hidden_act = (gate_act * up_pre).astype(jnp.bfloat16)
    d_up = (d_hidden * gate_act).astype(jnp.bfloat16)
    d_gate = (d_hidden * up_pre * gate_sigmoid * (1.0 + gate_pre * (1.0 - gate_sigmoid))).astype(
        jnp.bfloat16
    )
    dx_rows = jnp.dot(d_gate, w_gate, preferred_element_type=jnp.float32) + jnp.dot(
        d_up, w_up, preferred_element_type=jnp.float32
    )
    dx_slots, hidden_act, d_gate, d_up, x_slots, dy_slots = (
        dx_rows.reshape(lead_count, item_count, feat_width),
        hidden_act.reshape(lead_count, item_count, hidden),
        d_gate.reshape(lead_count, item_count, hidden),
        d_up.reshape(lead_count, item_count, hidden),
        x_slots,
        dy_slots,
    )
    returned = lax.all_to_all(
        dx_slots.astype(jnp.bfloat16), "expert", split_axis=0, concat_axis=0, tiled=True
    ).astype(dx_slots.dtype)
    dx_routes = jnp.take(returned.reshape(slot_total, feat_width), slot_index, axis=0)
    d_tokens = jnp.sum(dx_routes.reshape(tok_count, top_count, feat_width), axis=1).astype(
        jnp.bfloat16
    )
    x_rows = x_slots.reshape(slot_total, feat_width)
    dy_rows = dy_slots.reshape(slot_total, feat_width)
    gate_rows = d_gate.reshape(slot_total, hidden)
    up_rows = d_up.reshape(slot_total, hidden)
    act_rows = hidden_act.reshape(slot_total, hidden)

    def part_term(factor, operand):
        return contract_rows(factor, operand)

    grad_total = lax.psum_scatter(
        jnp.concatenate(
            [
                part_term(gate_rows, x_rows),
                part_term(up_rows, x_rows),
                part_term(act_rows, dy_rows),
            ],
            axis=1,
        ).astype(jnp.bfloat16),
        "replica",
        scatter_dimension=0,
        tiled=True,
    )
    g_stack = grad_total[None]
    return (d_tokens, g_stack)


def solution(mesh):
    return jax.shard_map(
        body,
        mesh=mesh,
        in_specs=(
            P(("expert", "replica"), None),
            P(("expert", "replica"), None),
            P(("expert", "replica"), None),
            P(("expert", "replica"), None),
            P("expert", None, None),
        ),
        out_specs=(P(("expert", "replica"), None), P("expert", "replica", None)),
        check_vma=False,
    )
```

profile of v0, /device:TPU:0, one launch (start us, length us, event | category | flops | bytes accessed | tf_op | source)
XLA Modules:
  0.0 271.1 jit_solution(15204027200174943964)
XLA Ops:
  9.2 1.7 broadcast_in_dim.24
  11.3 2.0 convolution_convert_fusion.3
  13.3 8.5 %all-to-all-start.1 = ((bf16[32,16,2048]{2,1,0:T(8,128)(2,1)}), bf16[32,16,2048]{2,1,0:T(8,128)(2,1)}, u32[]{:S(2)}, u32[]{:S(2)}) async-start(bf16[32,16,2048]{2,1,0:T(8,128)(2,1)} %bitcast.4), calls=%async_computation.1 | async-start | bytes 4194304 | tf_op jit(solution)/shard_map/all_to_all | solution.py:42
  23.2 2.5 convert_element_type.44
  25.7 3.7 %convolution_convert_fusion.4 = bf16[512,2048]{1,0:T(8,128)(2,1)} fusion(f32[256,2048]{1,0:T(8,128)} %convert_element_type.44, f32[256]{0:T(256)S(1)} %mul.66, s32[256]{0:T(256)S(1)} %multiply_add_fusion), kind=kOutput, calls=%fused_computation.17 | convolution fusion | flops 539099136 | bytes 4196352 | tf_op jit(solution)/shard_map/dot_general | solution.py:40
  29.4 22.4 %all-to-all-done.1 = bf16[32,16,2048]{2,1,0:T(8,128)(2,1)} async-done(((bf16[32,16,2048]{2,1,0:T(8,128)(2,1)}), bf16[32,16,2048]{2,1,0:T(8,128)(2,1)}, u32[]{:S(2)}, u32[]{:S(2)}) %all-to-all-start.1) | async-done | bytes 2097184 | tf_op jit(solution)/shard_map/all_to_all | solution.py:42
  51.8 4.0 %all-to-all-start = ((bf16[32,16,2048]{2,1,0:T(8,128)(2,1)}), bf16[32,16,2048]{2,1,0:T(8,128)(2,1)S(1)}, u32[]{:S(2)}, u32[]{:S(2)}) async-start(bf16[32,16,2048]{2,1,0:T(8,128)(2,1)} %bitcast.1), calls=%async_computation | async-start | bytes 4194304 | tf_op jit(solution)/shard_map/all_to_all | solution.py:43
  56.1 8.3 %fusion.4 = f32[512,1408]{1,0:T(8,128)} fusion(bf16[512,2048]{1,0:T(8,128)(2,1)} %bitcast.5, bf16[1408,6144]{1,0:T(8,128)(2,1)} %bitcast.43), kind=kOutput, calls=%fused_computation.9 | convolution fusion | flops 2952790016 | bytes 10747904 | tf_op jit(solution)/shard_map/dot_general | solution.py:48
  64.4 8.3 %fusion.8 = f32[512,1408]{1,0:T(8,128)} fusion(bf16[512,2048]{1,0:T(8,128)(2,1)} %bitcast.5, bf16[1408,6144]{1,0:T(8,128)(2,1)} %bitcast.44), kind=kOutput, calls=%fused_computation.13 | convolution fusion | flops 2952790016 | bytes 10747904 | tf_op jit(solution)/shard_map/dot_general | solution.py:49
  72.7 13.2 %all-to-all-done = bf16[32,16,2048]{2,1,0:T(8,128)(2,1)S(1)} async-done(((bf16[32,16,2048]{2,1,0:T(8,128)(2,1)}), bf16[32,16,2048]{2,1,0:T(8,128)(2,1)S(1)}, u32[]{:S(2)}, u32[]{:S(2)}) %all-to-all-start) | async-done | bytes 2097184 | tf_op jit(solution)/shard_map/all_to_all | solution.py:43
  85.8 8.6 %multiply_convert_fusion.1 = (bf16[512,1408]{1,0:T(8,128)(2,1)S(1)}, bf16[512,1408]{1,0:T(8,128)(2,1)S(1)}) fusion(f32[512,1408]{1,0:T(8,128)} %fusion.4, f32[512,1408]{1,0:T(8,128)} %fusion.8, bf16[512,2048]{1,0:T(8,128)(2,1)S(1)} %bitcast.39, bf16[1408,6144]{1,0:T(8,128)(2,1)} %bitcast.45), kind=kOutput, calls=%fused_computation.19 | convolution fusion | flops 2962161664 | bytes 16515072 | tf_op jit(solution)/shard_map/dot_general | solution.py:50
  94.5 3.8 %convolution_convert_fusion = bf16[1408,2048]{1,0:T(8,128)(2,1)S(1)} fusion(bf16[512,2048]{1,0:T(8,128)(2,1)S(1)} %bitcast.40, f32[512,1408]{1,0:T(8,128)S(1)} %copy-done.4, f32[512,1408]{1,0:T(8,128)S(1)} %copy-done.3), kind=kOutput, calls=%fused_computation.2 | convolution fusion | flops 2959998976 | bytes 13631488 | tf_op jit(solution)/shard_map/dot_general | solution.py:8
  98.3 4.8 %convolution_convert_fusion.1 = bf16[1408,2048]{1,0:T(8,128)(2,1)S(1)} fusion(bf16[512,1408]{1,0:T(8,128)(2,1)S(1)} %get-tuple-element.2, bf16[512,2048]{1,0:T(8,128)(2,1)} %bitcast.5), kind=kOutput, calls=%fused_computation.3 | convolution fusion | flops 2955673600 | bytes 9306112 | tf_op jit(solution)/shard_map/dot_general | solution.py:8
  103.1 4.8 %convolution_convert_fusion.2 = bf16[1408,2048]{1,0:T(8,128)(2,1)S(1)} fusion(bf16[512,1408]{1,0:T(8,128)(2,1)S(1)} %get-tuple-element.3, bf16[512,2048]{1,0:T(8,128)(2,1)} %bitcast.5), kind=kOutput, calls=%fused_computation.4 | convolution fusion | flops 2955673600 | bytes 9306112 | tf_op jit(solution)/shard_map/dot_general | solution.py:8
  107.9 6.8 %pad_maximum_fusion = bf16[1408,6144]{1,0:T(8,128)(2,1)} fusion(bf16[1408,2048]{1,0:T(8,128)(2,1)S(1)} %convolution_convert_fusion, bf16[1408,2048]{1,0:T(8,128)(2,1)S(1)} %convolution_convert_fusion.1, bf16[1408,2048]{1,0:T(8,128)(2,1)S(1)} %convolution_convert_fusion.2), kind=kLoop, calls=%fused_computation.1 | loop fusion | flops 51904512 | bytes 34603008 | tf_op jit(solution)/shard_map/concatenate | solution.py:86
  116.1 5.5 %fusion.2 = f32[512,2048]{1,0:T(8,128)S(1)} fusion(bf16[512,1408]{1,0:T(8,128)(2,1)S(1)} %copy-done.8, bf16[1408,6144]{1,0:T(8,128)(2,1)} %bitcast.46), kind=kOutput, calls=%fused_computation.7 | convolution fusion | flops 2952790016 | bytes 11403264 | tf_op jit(solution)/shard_map/dot_general | solution.py:58
  121.7 7.5 %add_convert_fusion = bf16[512,2048]{1,0:T(8,128)(2,1)} fusion(f32[512,2048]{1,0:T(8,128)S(1)} %fusion.2, bf16[512,1408]{1,0:T(8,128)(2,1)S(1)} %copy-done.6, bf16[1408,6144]{1,0:T(8,128)(2,1)} %bitcast.47), kind=kOutput, calls=%fused_computation.15 | convolution fusion | flops 2954887168 | bytes 13500416 | tf_op jit(solution)/shard_map/dot_general | solution.py:58
  129.2 4.4 %all-to-all-start.2 = ((bf16[32,16,2048]{2,1,0:T(8,128)(2,1)}), bf16[32,16,2048]{2,1,0:T(8,128)(2,1)S(1)}, u32[]{:S(2)}, u32[]{:S(2)}) async-start(bf16[32,16,2048]{2,1,0:T(8,128)(2,1)} %bitcast.38), calls=%async_computation.2 | async-start | bytes 4194304 | tf_op jit(solution)/shard_map/all_to_all | solution.py:69
  134.3 29.0 %all-to-all-done.2 = bf16[32,16,2048]{2,1,0:T(8,128)(2,1)S(1)} async-done(((bf16[32,16,2048]{2,1,0:T(8,128)(2,1)}), bf16[32,16,2048]{2,1,0:T(8,128)(2,1)S(1)}, u32[]{:S(2)}, u32[]{:S(2)}) %all-to-all-start.2) | async-done | bytes 2097184 | tf_op jit(solution)/shard_map/all_to_all | solution.py:69
  163.3 2.6 bitcast_convert_fusion
  165.9 4.6 %gather_fusion = f32[256,2048]{1,0:T(8,128)S(1)} fusion(f32[512,2048]{1,0:T(8,128)} %bitcast_convert_fusion, s32[1024]{0:T(1024)S(1)} %pad_clamp_fusion), kind=kCustom, calls=%fused_computation | custom fusion | bytes 4195328 | tf_op jit(solution)/shard_map/jit(_take)/gather | solution.py:72
  170.5 2.2 gather.7
  172.8 5.7 %select_reduce_fusion = bf16[128,2048]{1,0:T(8,128)(2,1)} fusion(f32[128,2,2048]{2,1,0:T(2,128)} %gather.7, pred[128,2]{1,0:T(8,128)(4,1)S(1)} %copy.17), kind=kLoop, calls=%fused_computation.24 | loop fusion | flops 786432 | bytes 2621696 | tf_op jit(solution)/shard_map/reduce_sum | solution.py:73
  178.5 85.8 %reduce-scatter.2.cloned.1.call-done = bf16[352,6144]{1,0:T(8,128)(2,1)} async-done(((bf16[1408,6144]{1,0:T(8,128)(2,1)}), bf16[352,6144]{1,0:T(8,128)(2,1)}) %reduce-scatter.2.cloned.1.call-update) | async-done | bytes 4325392 | tf_op jit(solution)/shard_map/reduce_scatter | solution.py:85
  (43 shorter events, 6.0 us)
Async XLA Ops:
  13.3 8.5 %copy-start.2 = (f32[128,2]{0,1:T(2,128)S(1)}, f32[128,2]{0,1:T(2,128)}, u32[]{:S(2)}) copy-start(f32[128,2]{0,1:T(2,128)} %param.8) | copy-start | bytes 3076
  13.3 8.8 %copy-start = (bf16[128,2048]{1,0:T(8,128)(2,1)S(1)}, bf16[128,2048]{1,0:T(8,128)(2,1)}, u32[]{:S(2)}) copy-start(bf16[128,2048]{1,0:T(8,128)(2,1)} %param.6) | copy-start | bytes 1572868
  13.3 38.5 %all-to-all-start.1 = ((bf16[32,16,2048]{2,1,0:T(8,128)(2,1)}), bf16[32,16,2048]{2,1,0:T(8,128)(2,1)}, u32[]{:S(2)}, u32[]{:S(2)}) async-start(bf16[32,16,2048]{2,1,0:T(8,128)(2,1)} %bitcast.4), calls=%async_computation.1 | async-start | bytes 4194304 | tf_op jit(solution)/shard_map/all_to_all | solution.py:42
  51.8 34.0 %all-to-all-start = ((bf16[32,16,2048]{2,1,0:T(8,128)(2,1)}), bf16[32,16,2048]{2,1,0:T(8,128)(2,1)S(1)}, u32[]{:S(2)}, u32[]{:S(2)}) async-start(bf16[32,16,2048]{2,1,0:T(8,128)(2,1)} %bitcast.1), calls=%async_computation | async-start | bytes 4194304 | tf_op jit(solution)/shard_map/all_to_all | solution.py:43
  55.9 208.4 %reduce-scatter.2.cloned.1.call-start = ((), (), s32[]{:S(2)}) async-start(), calls=%async_computation.4 | async-start | bytes 21626880 | tf_op jit(solution)/shard_map/reduce_scatter | solution.py:85
  85.8 8.6 %copy-start.3 = (f32[512,1408]{1,0:T(8,128)S(1)}, f32[512,1408]{1,0:T(8,128)}, u32[]{:S(2)}) copy-start(f32[512,1408]{1,0:T(8,128)} %fusion.4) | copy-start | bytes 8650756
  85.8 8.6 %copy-start.4 = (f32[512,1408]{1,0:T(8,128)S(1)}, f32[512,1408]{1,0:T(8,128)}, u32[]{:S(2)}) copy-start(f32[512,1408]{1,0:T(8,128)} %fusion.8) | copy-start | bytes 8650756
  94.5 3.8 %copy-start.5 = (bf16[512,1408]{1,0:T(8,128)(2,1)}, bf16[512,1408]{1,0:T(8,128)(2,1)S(1)}, u32[]{:S(2)}) copy-start(bf16[512,1408]{1,0:T(8,128)(2,1)S(1)} %get-tuple-element.2) | copy-start | bytes 4325380
  94.5 8.6 %copy-start.7 = (bf16[512,1408]{1,0:T(8,128)(2,1)}, bf16[512,1408]{1,0:T(8,128)(2,1)S(1)}, u32[]{:S(2)}) copy-start(bf16[512,1408]{1,0:T(8,128)(2,1)S(1)} %get-tuple-element.3) | copy-start | bytes 4325380
  114.7 1.4 copy-start.8
  116.1 5.6 %copy-start.6 = (bf16[512,1408]{1,0:T(8,128)(2,1)S(1)}, bf16[512,1408]{1,0:T(8,128)(2,1)}, u32[]{:S(2)}) copy-start(bf16[512,1408]{1,0:T(8,128)(2,1)} %copy-done.5) | copy-start | bytes 4325380
  129.2 4.6 %copy-start.1 = (s32[128,2]{0,1:T(2,128)S(1)}, s32[128,2]{0,1:T(2,128)}, u32[]{:S(2)}) copy-start(s32[128,2]{0,1:T(2,128)} %param.7) | copy-start | bytes 3076
  129.2 34.1 %all-to-all-start.2 = ((bf16[32,16,2048]{2,1,0:T(8,128)(2,1)}), bf16[32,16,2048]{2,1,0:T(8,128)(2,1)S(1)}, u32[]{:S(2)}, u32[]{:S(2)}) async-start(bf16[32,16,2048]{2,1,0:T(8,128)(2,1)} %bitcast.38), calls=%async_computation.2 | async-start | bytes 4194304 | tf_op jit(solution)/shard_map/all_to_all | solution.py:69
Sparse Core Ops, SparseCore 0:
  114.9 149.3 reduce-scatter.1
where the time goes:
time: 273 us; the launch traced here: 271 us
  waiting for transfers between devices  150 us (55%)
  matrix products  57.4 us (21%)
  starting transfers between devices  17.2 us (6%)
  local copies, waits for them, and re-layouts  15.9 us (6%)
  other arithmetic  15.9 us (6%)
  between operations  14.3 us (5%)
    reduce_scatter x1, waiting for transfers between devices, body(): lax.psum_scatter(jnp.concatenate([part_term(gate_rows, x_rows), part_term...  85.8 us
    all_to_all x1, waiting for transfers between devices, body(): lax.all_to_all(dx_slots.astype(jnp.bfloat16), 'expert', split_axis=0, con...  29 us
    all_to_all x1, waiting for transfers between devices, body(): lax.all_to_all(send_x, 'expert', split_axis=0, concat_axis=0, tiled=True)  22.4 us
    dot_general x3, matrix products, contract_rows(): lax.dot_general(factor, operand, (((0,), (0,)), ((), ())), preferred_elem...  13.4 us
    all_to_all x1, waiting for transfers between devices, body(): lax.all_to_all(send_dy, 'expert', split_axis=0, concat_axis=0, tiled=True)  13.2 us
    dot_general x1, matrix products, body(): lax.dot_general(grads_in, w_down, last_dims, preferred_element_type=jnp.f...  8.62 us
    all_to_all x1, starting transfers between devices, body(): lax.all_to_all(send_x, 'expert', split_axis=0, concat_axis=0, tiled=True)  8.51 us
    dot_general x1, matrix products, body(): lax.dot_general(row_block, w_gate, last_dims, preferred_element_type=jnp....  8.3 us
  transfers between devices with their start and end apart: 4, of which 4 were waited for; matrix products, arithmetic and copies ran while one was open for 20% of the time, Pallas kernels for 0%

commit v1 on v0

v1 whole, which is shorter than its diff:
```python
import functools

import jax
import jax.numpy as jnp
from jax import lax
from jax.experimental import pallas as pl
from jax.experimental.pallas import tpu as pltpu
from jax.sharding import PartitionSpec as P

MESH = pl.DeviceIdType.MESH
PARTS = 4
OFFSETS = [
    (2, 2), (1, 1), (3, 3), (1, 3), (3, 1), (2, 1), (1, 2), (2, 3),
    (3, 2), (2, 0), (0, 2), (1, 0), (0, 1), (3, 0), (0, 3), (0, 0),
]


def step_of(expert, group):
    return 1 - 2 * ((group + expert) % 2)


def dispatch_kernel(peers, groups, send_ref, own_ref, mate_ref, send_sem, recv_sem, keep_sem, pass_sem, take_sem):
    e = lax.axis_index("expert")
    r = lax.axis_index("replica")
    mate = lax.rem(r + groups + step_of(e, r), groups)
    arrays, width = send_ref.shape[0], send_ref.shape[-1] // PARTS
    total = arrays * PARTS

    barrier = pltpu.get_barrier_semaphore()
    for k in range(1, peers):
        pl.semaphore_signal(barrier, inc=1, device_id=((e + k) % peers, r), device_id_type=MESH)
    pl.semaphore_signal(barrier, inc=1, device_id=(e, mate), device_id_type=MESH)
    pl.semaphore_wait(barrier, peers)

    z, x, c = e // 8, (e // 2) % 4, e % 2
    order = [
        ((z + dz) % 4) * 8 + ((x + dx) % 4) * 2 + (c + dc) % 2
        for dz, dx in OFFSETS
        for dc in (0, 1)
        if (dz, dx, dc) != (0, 0, 0)
    ]

    def place(k):
        return k // PARTS, pl.ds((k % PARTS) * width, width)

    def keep(k):
        a, cols = place(k)
        return pltpu.make_async_copy(send_ref.at[a, e, :, cols], own_ref.at[a, e, :, cols], keep_sem.at[k])

    def remote(k, src, dst, send, recv, device):
        return pltpu.make_async_remote_copy(
            src_ref=src, dst_ref=dst, send_sem=send.at[k], recv_sem=recv.at[k], device_id=device, device_id_type=MESH
        )

    def everyone(k):
        a, cols = place(k)
        some = pl.ds(0, peers - 1)
        return remote(k, send_ref.at[a, some, :, cols], own_ref.at[a, some, :, cols], send_sem, recv_sem, (e, mate))

    def across(k):
        a, cols = place(k)
        return remote(k, own_ref.at[a, :, :, cols], mate_ref.at[a, :, :, cols], pass_sem, take_sem, (e, mate))

    for k in range(total + 1):
        if k < total:
            a, cols = place(k)
            for to in order:
                remote(k, send_ref.at[a, to, :, cols], own_ref.at[a, e, :, cols], send_sem, recv_sem, (to, r)).start()
            keep(k).start()
        if k > 0:
            everyone(k - 1).wait_recv()
            keep(k - 1).wait()
            across(k - 1).start()
    for k in range(total):
        everyone(k).wait_send()
        across(k).wait()


def dispatch(send, groups):
    shape = jax.ShapeDtypeStruct(send.shape, send.dtype)
    return pl.pallas_call(
        functools.partial(dispatch_kernel, send.shape[1], groups),
        out_shape=(shape, shape),
        in_specs=[pl.BlockSpec(memory_space=pltpu.VMEM)],
        out_specs=(pl.BlockSpec(memory_space=pl.ANY),) * 2,
        scratch_shapes=[pltpu.SemaphoreType.DMA((send.shape[0] * PARTS,))] * 5,
        compiler_params=pltpu.CompilerParams(
            collective_id=0, has_side_effects=True, vmem_limit_bytes=40 * 1024 * 1024
        ),
        name="dispatch",
    )(send)


def rows_by_rows(left, right):
    return lax.dot_general(left, right, (((1,), (1,)), ((), ())), preferred_element_type=jnp.float32)


def forward(weights, x, dy, width):
    gate = rows_by_rows(weights[:, :width], x)
    up = rows_by_rows(weights[:, width : 2 * width], x)
    d_hidden = rows_by_rows(weights[:, 2 * width :], dy)
    s = jax.nn.sigmoid(gate)
    act = gate * s
    hidden = (act * up).astype(jnp.bfloat16)
    d_up = (d_hidden * act).astype(jnp.bfloat16)
    d_gate = (d_hidden * up * s * (1.0 + gate * (1.0 - s))).astype(jnp.bfloat16)
    return hidden, d_gate, d_up


def weight_grad(acts, x, dy):
    hidden, d_gate, d_up = acts
    dot = functools.partial(jnp.dot, preferred_element_type=jnp.float32)
    return jnp.concatenate([dot(d_gate, x), dot(d_up, x), dot(hidden, dy)], axis=1)


def body(x_tokens, d_out, expert_ids, combine, w_stack):
    tokens, width = x_tokens.shape
    experts, groups = lax.axis_size("expert"), lax.axis_size("replica")
    capacity = 2 * tokens * expert_ids.shape[1] // experts
    slots = experts * capacity
    e, r = lax.axis_index("expert"), lax.axis_index("replica")
    other = (r + groups - step_of(e, r)) % groups

    ids = expert_ids.T
    iota = jnp.arange(experts, dtype=jnp.int32)
    member = [(ids[k][:, None] == iota[None, :]).astype(jnp.float32) for k in range(ids.shape[0])]
    both = functools.reduce(jnp.add, member)
    lower = (jnp.arange(tokens)[:, None] > jnp.arange(tokens)[None, :]).astype(jnp.float32)
    before = jnp.dot(lower, both, preferred_element_type=jnp.float32)
    slot = jnp.stack(
        [ids[k] * capacity + jnp.sum(before * member[k], axis=1).astype(jnp.int32) for k in range(ids.shape[0])]
    )
    places = [jnp.arange(slots, dtype=jnp.int32)[:, None] == slot[k][None, :] for k in range(ids.shape[0])]
    place = functools.reduce(jnp.logical_or, places).astype(jnp.bfloat16)
    scale = sum(jnp.sum(jnp.where(places[k], combine[:, k][None, :], 0.0), axis=1) for k in range(ids.shape[0]))
    send_x = jnp.dot(place, x_tokens, preferred_element_type=jnp.float32).astype(jnp.bfloat16)
    send_dy = (scale[:, None] * jnp.dot(place, d_out, preferred_element_type=jnp.float32)).astype(jnp.bfloat16)
    send = jnp.stack([send_x, send_dy]).reshape(2, experts, capacity, width)

    own, mate = dispatch(send, groups)
    own, mate = own.reshape(2, slots, width), mate.reshape(2, slots, width)
    weights = w_stack[0]
    hidden = weights.shape[0]
    shard = hidden // groups

    w_other = lax.dynamic_slice_in_dim(weights, other * shard, shard, 0)
    w_mine = lax.dynamic_slice_in_dim(weights, r * shard, shard, 0)

    def both_planes(w):
        a, b = forward(w, own[0], own[1], width), forward(w, mate[0], mate[1], width)
        ga, gb = weight_grad(a, own[0], own[1]), weight_grad(b, mate[0], mate[1])
        return ga + gb

    pairs = []
    for i in range(experts):
        for g in range(groups):
            pairs.append((i * groups + g, i * groups + (g - step_of(i, g)) % groups))
    partial = both_planes(w_other).astype(jnp.bfloat16)
    theirs = lax.ppermute(partial, ("expert", "replica"), pairs)
    own, mate, partial = lax.optimization_barrier((own, mate, partial))

    _, d_gate, d_up = forward(weights, own[0], own[1], width)
    rows = (((0,), (0,)), ((), ()))
    dx = lax.dot_general(d_gate, weights[:, :width], rows, preferred_element_type=jnp.float32) + lax.dot_general(
        d_up, weights[:, width : 2 * width], rows, preferred_element_type=jnp.float32
    )
    dx = dx.astype(jnp.bfloat16)
    own, mate, dx = lax.optimization_barrier((own, mate, dx))
    back = lax.all_to_all(
        dx.reshape(experts, capacity, width), "expert", split_axis=0, concat_axis=0, tiled=True
    )
    d_tokens = lax.dot_general(
        place, back.reshape(slots, width), rows, preferred_element_type=jnp.float32
    ).astype(jnp.bfloat16)

    mine = both_planes(w_mine)
    g_stack = (mine + theirs.astype(jnp.float32)).astype(jnp.bfloat16)
    return d_tokens, g_stack[None]


def solution(mesh):
    rows = P(("expert", "replica"), None)
    return jax.shard_map(
        body,
        mesh=mesh,
        in_specs=(rows, rows, rows, rows, P("expert", None, None)),
        out_specs=(rows, P("expert", "replica", None)),
        check_vma=False,
    )
```

time: 273 us -> 206 us (0.75)
  waiting for transfers between devices: 150 us -> 3.11 us
  Pallas kernels: 0 us -> 63.1 us
  matrix products: 57.4 us -> 91.1 us
  between operations: 14.3 us -> 1.16 us
  starting transfers between devices: 17.2 us -> 7.48 us
    reduce_scatter x1 -> x0, waiting for transfers between devices: 85.8 us -> none  [body(): lax.psum_scatter(jnp.concatenate([part_term(gate_rows, x_rows), part_term...]
    pallas_call x0 -> x1, Pallas kernels: none -> 63.1 us  [dispatch(): pl.pallas_call(functools.partial(dispatch_kernel, send.shape[1], groups),...]
    all_to_all x3 -> x1, waiting for transfers between devices: 64.6 us -> 3.11 us  [body(): lax.all_to_all(dx.reshape(experts, capacity, width), 'expert', split_axis...]
    dot_general x10 -> x32, matrix products: 57.4 us -> 91.1 us  [the longest x14 32.4 us: rows_by_rows(): lax.dot_general(left, right, (((1,), (1,)), ((), ())), preferred_element_...]
    all_to_all x3 -> x1, starting transfers between devices: 16.9 us -> 5.14 us  [body(): lax.all_to_all(dx.reshape(experts, capacity, width), 'expert', split_axis...]
    broadcast_in_dim x0 -> x1, other arithmetic: none -> 10.2 us  [body(): return (d_tokens, g_stack[None])]
    dynamic_slice x0 -> x1, local copies, waits for them, and re-layouts: none -> 7.41 us  [body(): w_mine = lax.dynamic_slice_in_dim(weights, r * shard, shard, 0)]
    gather x2 -> x0, local copies, waits for them, and re-layouts: 6.84 us -> none  [body(): jnp.take(returned.reshape(slot_total, feat_width), slot_index, axis=0)]
  transfers between devices with their start and end apart: 4 -> 2, of which waited for: 4 -> 1; matrix products, arithmetic and copies ran while one was open for 20% -> 34% of each run, Pallas kernels for 0% -> 0%
where the time goes in v1:
time: 206 us; the launch traced here: 202 us
  matrix products  91.1 us (44%)
  Pallas kernels  63.1 us (31%)
  other arithmetic  18.2 us (9%)
  local copies, waits for them, and re-layouts  17.8 us (9%)
  starting transfers between devices  7.48 us (4%)
  waiting for transfers between devices  3.11 us (2%)
    pallas_call x1, Pallas kernels, dispatch(): pl.pallas_call(functools.partial(dispatch_kernel, send.shape[1], groups),...  63.1 us
    dot_general x14, matrix products, rows_by_rows(): lax.dot_general(left, right, (((1,), (1,)), ((), ())), preferred_element_...  32.4 us
    dot_general x1, matrix products, body(): lax.dot_general(d_gate, weights[:, :width], rows, preferred_element_type=...  15.7 us
    dot_general x4, matrix products, weight_grad(): dot(d_gate, x)  10.6 us
    dot_general x1, matrix products, body(): lax.dot_general(d_up, weights[:, width:2 * width], rows, preferred_elemen...  10.6 us
    dot_general x4, matrix products, weight_grad(): dot(d_up, x)  10.3 us
    broadcast_in_dim x1, other arithmetic, body(): return (d_tokens, g_stack[None])  10.2 us
    dot_general x4, matrix products, weight_grad(): dot(hidden, dy)  8.62 us
  transfers between devices with their start and end apart: 2, of which 1 were waited for; matrix products, arithmetic and copies ran while one was open for 34% of the time, Pallas kernels for 0%

profile of v1, /device:TPU:0, one launch (start us, length us, event | category | flops | bytes accessed | tf_op | source)
XLA Modules:
  0.0 201.9 jit_solution(258267056868945608)
XLA Ops:
  5.2 63.1 %dispatch.1 = (bf16[2,32,16,2048]{3,2,1,0:T(8,128)(2,1)S(1)}, bf16[2,32,16,2048]{3,2,1,0:T(8,128)(2,1)S(1)}) custom-call(bf16[2,32,16,2048]{3,2,1,0:T(8,128)(2,1)S(1)} %pad_maximum_fusion.send_ref), custom_call_target="tpu_custom_call" | custom-call | tf_op jit(solution)/shard_map/dispatch/pallas_call | solution.py:81
  74.0 7.4 %dynamic-slice_bitcast_fusion = (bf16[352,6144]{1,0:T(8,128)(2,1)}, bf16[352,6144]{1,0:T(8,128)(2,1)S(1)}) fusion(bf16[1,1408,6144]{2,1,0:T(8,128)(2,1)} %param.9, s32[]{:T(128)S(6)} %select_n.29, s32[]{:T(128)S(6)} %select_n.28), kind=kLoop, calls=%fused_computation.15 | loop fusion | bytes 17301512 | tf_op jit(solution)/shard_map/dynamic_slice | solution.py:147
  90.3 2.6 %fusion.111 = f32[352,2048]{1,0:T(8,128)} fusion(bf16[512,2048]{1,0:T(8,128)(2,1)S(1)} %bitcast.134, f32[352,512]{1,0:T(8,128)S(1)} %fusion.92, f32[352,512]{1,0:T(8,128)S(1)} %fusion.100, f32[352,512]{1,0:T(8,128)S(1)} %fusion.96), kind=kOutput, calls=%fused_computation.117 | convolution fusion | flops 739999744 | bytes 7143424 | tf_op jit(solution)/shard_map/dot_general | solution.py:113
  92.9 2.6 %fusion.112 = f32[352,2048]{1,0:T(8,128)} fusion(bf16[512,2048]{1,0:T(8,128)(2,1)S(1)} %bitcast.135, f32[352,512]{1,0:T(8,128)S(1)} %fusion.100, f32[352,512]{1,0:T(8,128)S(1)} %fusion.92), kind=kOutput, calls=%fused_computation.118 | convolution fusion | flops 739278848 | bytes 6422528 | tf_op jit(solution)/shard_map/dot_general | solution.py:113
  96.6 2.6 %fusion.110 = f32[352,2048]{1,0:T(8,128)} fusion(bf16[512,2048]{1,0:T(8,128)(2,1)S(1)} %bitcast.143, f32[352,512]{1,0:T(8,128)S(1)} %fusion.98, f32[352,512]{1,0:T(8,128)S(1)} %fusion.94), kind=kOutput, calls=%fused_computation.116 | convolution fusion | flops 739278848 | bytes 6422528 | tf_op jit(solution)/shard_map/dot_general | solution.py:113
  99.1 2.7 %fusion.108 = f32[352,2048]{1,0:T(8,128)} fusion(bf16[512,2048]{1,0:T(8,128)(2,1)S(1)} %bitcast.140, f32[352,512]{1,0:T(8,128)S(1)} %fusion.94, f32[352,512]{1,0:T(8,128)S(1)} %fusion.102, f32[352,512]{1,0:T(8,128)S(1)} %fusion.98), kind=kOutput, calls=%fused_computation.114 | convolution fusion | flops 739999744 | bytes 7143424 | tf_op jit(solution)/shard_map/dot_general | solution.py:113
  101.9 2.6 %fusion.109 = f32[352,2048]{1,0:T(8,128)} fusion(bf16[512,2048]{1,0:T(8,128)(2,1)S(1)} %bitcast.141, f32[352,512]{1,0:T(8,128)S(1)} %fusion.102, f32[352,512]{1,0:T(8,128)S(1)} %fusion.94), kind=kOutput, calls=%fused_computation.115 | convolution fusion | flops 739278848 | bytes 6422528 | tf_op jit(solution)/shard_map/dot_general | solution.py:113
  104.4 6.6 %fusion = bf16[352,6144]{1,0:T(8,128)(2,1)} fusion(f32[352,2048]{1,0:T(8,128)} %fusion.110, f32[352,2048]{1,0:T(8,128)} %fusion.109, f32[352,2048]{1,0:T(8,128)} %fusion.108, f32[352,2048]{1,0:T(8,128)S(1)} %fusion.113, f32[352,2048]{1,0:T(8,128)} %fusion.112, f32[352,2048]{1,0:T(8,128)S(1)} %copy-done.7), kind=kLoop, calls=%fused_computation.1 | loop fusion | flops 12976128 | bytes 21626880 | tf_op jit(solution)/shard_map/convert_element_type | solution.py:158
  113.4 7.7 %fusion.26 = f32[1408,512]{0,1:T(8,128)} fusion(bf16[1408,6144]{1,0:T(8,128)(2,1)} %bitcast.125, bf16[2,512,2048]{2,1,0:T(8,128)(2,1)S(1)} %bitcast.109), kind=kOutput, calls=%fused_computation.25 | convolution fusion | flops 2952790016 | bytes 10747904 | tf_op jit(solution)/shard_map/dot_general | solution.py:95
  121.1 7.7 %fusion.29 = f32[1408,512]{0,1:T(8,128)} fusion(bf16[1408,6144]{1,0:T(8,128)(2,1)} %bitcast.126, bf16[2,512,2048]{2,1,0:T(8,128)(2,1)S(1)} %bitcast.110), kind=kOutput, calls=%fused_computation.26 | convolution fusion | flops 2952790016 | bytes 10747904 | tf_op jit(solution)/shard_map/dot_general | solution.py:95
  128.7 15.7 %fusion.5 = f32[512,2048]{1,0:T(8,128)} fusion(bf16[1408,6144]{1,0:T(8,128)(2,1)} %bitcast.127, f32[1408,512]{0,1:T(8,128)} %fusion.29, f32[1408,512]{0,1:T(8,128)} %fusion.26, bf16[2,512,2048]{2,1,0:T(8,128)(2,1)} %bitcast.107), kind=kOutput, calls=%fused_computation.7 | convolution fusion | flops 5912788992 | bytes 23592960 | tf_op jit(solution)/shard_map/dot_general | solution.py:164
  144.5 10.6 %add_convert_fusion = bf16[512,2048]{1,0:T(8,128)(2,1)} fusion(f32[512,2048]{1,0:T(8,128)} %fusion.5, bf16[1408,6144]{1,0:T(8,128)(2,1)} %bitcast.128, f32[1408,512]{0,1:T(8,128)} %fusion.29, f32[1408,512]{0,1:T(8,128)} %fusion.26), kind=kOutput, calls=%fused_computation.19 | convolution fusion | flops 2959212544 | bytes 17825792 | tf_op jit(solution)/shard_map/dot_general | solution.py:164
  155.0 5.1 %all-to-all-start = ((bf16[32,16,2048]{2,1,0:T(8,128)(2,1)}), bf16[32,16,2048]{2,1,0:T(8,128)(2,1)S(1)}, u32[]{:S(2)}, u32[]{:S(2)}) async-start(bf16[32,16,2048]{2,1,0:T(8,128)(2,1)} %bitcast.131), calls=%async_computation | async-start | bytes 4194304 | tf_op jit(solution)/shard_map/all_to_all | solution.py:169
  160.2 3.1 %fusion.53 = f32[352,512]{1,0:T(8,128)S(1)} fusion(bf16[2,512,2048]{2,1,0:T(8,128)(2,1)} %bitcast.108, bf16[352,6144]{1,0:T(8,128)(2,1)} %get-tuple-element.18), kind=kOutput, calls=%fused_computation.48 | convolution fusion | flops 738197504 | bytes 4259840 | tf_op jit(solution)/shard_map/dot_general | solution.py:95
  163.4 2.6 %fusion.55 = f32[352,512]{1,0:T(8,128)S(1)} fusion(bf16[2,512,2048]{2,1,0:T(8,128)(2,1)S(1)} %bitcast.111, bf16[352,6144]{1,0:T(8,128)(2,1)} %get-tuple-element.18), kind=kOutput, calls=%fused_computation.50 | convolution fusion | flops 738197504 | bytes 4259840 | tf_op jit(solution)/shard_map/dot_general | solution.py:95
  166.0 2.5 %fusion.59 = f32[352,512]{1,0:T(8,128)S(1)} fusion(bf16[2,512,2048]{2,1,0:T(8,128)(2,1)S(1)} %bitcast.112, bf16[352,6144]{1,0:T(8,128)(2,1)} %get-tuple-element.18), kind=kOutput, calls=%fused_computation.54 | convolution fusion | flops 738197504 | bytes 4259840 | tf_op jit(solution)/shard_map/dot_general | solution.py:95
  170.5 2.6 %fusion.37 = f32[352,2048]{1,0:T(8,128)} fusion(bf16[2,512,2048]{2,1,0:T(8,128)(2,1)S(1)} %bitcast.118, f32[352,512]{1,0:T(8,128)S(1)} %fusion.47, f32[352,512]{1,0:T(8,128)S(1)} %fusion.41), kind=kOutput, calls=%fused_computation.32 | convolution fusion | flops 739278848 | bytes 6422528 | tf_op jit(solution)/shard_map/dot_general | solution.py:113
  174.1 2.6 %fusion.45 = f32[352,2048]{1,0:T(8,128)} fusion(bf16[2,512,2048]{2,1,0:T(8,128)(2,1)S(1)} %bitcast.120, f32[352,512]{1,0:T(8,128)S(1)} %fusion.43, f32[352,512]{1,0:T(8,128)S(1)} %fusion.41), kind=kOutput, calls=%fused_computation.40 | convolution fusion | flops 739278848 | bytes 6422528 | tf_op jit(solution)/shard_map/dot_general | solution.py:113
  176.7 2.5 %fusion.49 = f32[352,2048]{1,0:T(8,128)} fusion(bf16[2,512,2048]{2,1,0:T(8,128)(2,1)S(1)} %bitcast.113, f32[352,512]{1,0:T(8,128)S(1)} %fusion.59, f32[352,512]{1,0:T(8,128)S(1)} %fusion.53), kind=kOutput, calls=%fused_computation.44 | convolution fusion | flops 739278848 | bytes 6422528 | tf_op jit(solution)/shard_map/dot_general | solution.py:113
  179.3 2.5 %fusion.57 = f32[352,2048]{1,0:T(8,128)} fusion(bf16[2,512,2048]{2,1,0:T(8,128)(2,1)S(1)} %bitcast.114, f32[352,512]{1,0:T(8,128)S(1)} %fusion.55, f32[352,512]{1,0:T(8,128)S(1)} %fusion.53), kind=kOutput, calls=%fused_computation.52 | convolution fusion | flops 739278848 | bytes 6422528 | tf_op jit(solution)/shard_map/dot_general | solution.py:113
  181.8 2.6 %fusion.39 = f32[352,2048]{1,0:T(8,128)} fusion(bf16[2,512,2048]{2,1,0:T(8,128)(2,1)S(1)} %bitcast.121, f32[352,512]{1,0:T(8,128)S(1)} %fusion.41, f32[352,512]{1,0:T(8,128)S(1)} %fusion.47, f32[352,512]{1,0:T(8,128)S(1)} %fusion.43), kind=kOutput, calls=%fused_computation.34 | convolution fusion | flops 739999744 | bytes 7143424 | tf_op jit(solution)/shard_map/dot_general | solution.py:113
  184.4 2.7 %fusion.51 = f32[352,2048]{1,0:T(8,128)} fusion(bf16[2,512,2048]{2,1,0:T(8,128)(2,1)S(1)} %bitcast.115, f32[352,512]{1,0:T(8,128)S(1)} %fusion.53, f32[352,512]{1,0:T(8,128)S(1)} %fusion.59, f32[352,512]{1,0:T(8,128)S(1)} %fusion.55), kind=kOutput, calls=%fused_computation.46 | convolution fusion | flops 739999744 | bytes 7143424 | tf_op jit(solution)/shard_map/dot_general | solution.py:113
  187.0 3.1 %all-to-all-done = bf16[32,16,2048]{2,1,0:T(8,128)(2,1)S(1)} async-done(((bf16[32,16,2048]{2,1,0:T(8,128)(2,1)}), bf16[32,16,2048]{2,1,0:T(8,128)(2,1)S(1)}, u32[]{:S(2)}, u32[]{:S(2)}) %all-to-all-start) | async-done | bytes 2097184 | tf_op jit(solution)/shard_map/all_to_all | solution.py:169
  191.4 10.2 %fusion.13 = bf16[1,352,6144]{2,1,0:T(8,128)(2,1)} fusion(bf16[352,6144]{1,0:T(8,128)(2,1)} %collective-permute-done, f32[352,2048]{1,0:T(8,128)} %fusion.45, f32[352,2048]{1,0:T(8,128)} %fusion.37, f32[352,2048]{1,0:T(8,128)} %fusion.39, f32[352,2048]{1,0:T(8,128)} %fusion.57, f32[352,2048]{1,0:T(8,128)} %fusion.49, f32[352,2048]{1,0:T(8,128)} %fusion.51), kind=kLoop, calls=%fused_computation.17 | loop fusion | flops 17301504 | bytes 25952256 | tf_op jit(solution)/shard_map/broadcast_in_dim | solution.py:178
  (53 shorter events, 26.7 us)
Async XLA Ops:
  0.6 2.5 %copy-start = (bf16[128,2048]{1,0:T(8,128)(2,1)S(1)}, bf16[128,2048]{1,0:T(8,128)(2,1)}, u32[]{:S(2)}) copy-start(bf16[128,2048]{1,0:T(8,128)(2,1)} %param.5) | copy-start | bytes 1572868
  0.6 3.4 %copy-start.11 = (bf16[128,2048]{1,0:T(8,128)(2,1)S(1)}, bf16[128,2048]{1,0:T(8,128)(2,1)}, u32[]{:S(2)}) copy-start(bf16[128,2048]{1,0:T(8,128)(2,1)} %param.6) | copy-start | bytes 1572868
  68.3 2.0 copy-start.2
  70.3 1.9 copy-start.5
  74.0 8.4 %copy-start.8 = (bf16[1,32,16,2048]{3,2,1,0:T(8,128)(2,1)}, bf16[1,32,16,2048]{3,2,1,0:T(8,128)(2,1)S(1)}, u32[]{:S(2)}) copy-start(bf16[1,32,16,2048]{3,2,1,0:T(8,128)(2,1)S(1)} %get-tuple-element.20) | copy-start | bytes 6291460
  82.4 2.2 %copy-start.3 = (bf16[2,32,16,2048]{3,2,1,0:T(8,128)(2,1)S(1)}, bf16[2,32,16,2048]{3,2,1,0:T(8,128)(2,1)}, u32[]{:S(2)}) copy-start(bf16[2,32,16,2048]{3,2,1,0:T(8,128)(2,1)} %copy-done.2) | copy-start | bytes 12582916
  86.1 1.6 copy-start.10
  88.7 1.6 copy-start.9
  101.8 2.6 %copy-start.7 = (f32[352,2048]{1,0:T(8,128)S(1)}, f32[352,2048]{1,0:T(8,128)}, u32[]{:S(2)}) copy-start(f32[352,2048]{1,0:T(8,128)} %fusion.111) | copy-start | bytes 8650756
  111.0 80.4 %collective-permute-start = (bf16[352,6144]{1,0:T(8,128)(2,1)}, bf16[352,6144]{1,0:T(8,128)(2,1)}, u32[]{:S(2)}, u32[]{:S(2)}) collective-permute-start(bf16[352,6144]{1,0:T(8,128)(2,1)} %fusion), channel_id=1, source_target_pairs={{0,3},{1,2},{2,1},{3,0},{4,5},{5,4},{6,7},{7,6},{8,11},{9,10},{10,... | collective-permute-start | bytes 12976136 | tf_op jit(solution)/shard_map/ppermute | solution.py:159
  155.0 35.1 %all-to-all-start = ((bf16[32,16,2048]{2,1,0:T(8,128)(2,1)}), bf16[32,16,2048]{2,1,0:T(8,128)(2,1)S(1)}, u32[]{:S(2)}, u32[]{:S(2)}) async-start(bf16[32,16,2048]{2,1,0:T(8,128)(2,1)} %bitcast.131), calls=%async_computation | async-start | bytes 4194304 | tf_op jit(solution)/shard_map/all_to_all | solution.py:169
  160.2 3.3 %copy-start.4 = (bf16[2,32,16,2048]{3,2,1,0:T(8,128)(2,1)S(1)}, bf16[2,32,16,2048]{3,2,1,0:T(8,128)(2,1)}, u32[]{:S(2)}) copy-start(bf16[2,32,16,2048]{3,2,1,0:T(8,128)(2,1)} %copy-done.2) | copy-start | bytes 12582916
  160.2 8.3 %slice-start = ((s8[4325376]{0:T(1024)(128)(4,1)}), s8[4194304]{0:T(1024)(128)(4,1)S(1)}, s32[]{:S(2)}) async-start(s8[4325376]{0:T(1024)(128)(4,1)} %bitcast.129), calls=%async_computation.1 | async-start | bytes 8388608
  163.4 5.1 %slice-start.1 = ((s8[4325376]{0:T(1024)(128)(4,1)}), s8[131072]{0:T(1024)(128)(4,1)S(1)}, s32[]{:S(2)}) async-start(s8[4325376]{0:T(1024)(128)(4,1)} %bitcast.129), calls=%async_computation.2 | async-start | bytes 262144
  166.0 2.6 %copy-start.6 = (bf16[2,32,16,2048]{3,2,1,0:T(8,128)(2,1)S(1)}, bf16[2,32,16,2048]{3,2,1,0:T(8,128)(2,1)}, u32[]{:S(2)}) copy-start(bf16[2,32,16,2048]{3,2,1,0:T(8,128)(2,1)} %copy-done.5) | copy-start | bytes 12582916
  191.4 10.2 %copy-start.1 = (bf16[128,2048]{1,0:T(8,128)(2,1)S(1)}, bf16[128,2048]{1,0:T(8,128)(2,1)}, u32[]{:S(2)}) copy-start(bf16[128,2048]{1,0:T(8,128)(2,1)} %param.5) | copy-start | bytes 1572868

commit v2 on v1

--- a/solution.py
+++ b/solution.py
@@ -91,26 +91,208 @@
     )(send)
 
 
-def rows_by_rows(left, right):
-    return lax.dot_general(left, right, (((1,), (1,)), ((), ())), preferred_element_type=jnp.float32)
-
-
-def forward(weights, x, dy, width):
-    gate = rows_by_rows(weights[:, :width], x)
-    up = rows_by_rows(weights[:, width : 2 * width], x)
-    d_hidden = rows_by_rows(weights[:, 2 * width :], dy)
-    s = jax.nn.sigmoid(gate)
-    act = gate * s
-    hidden = (act * up).astype(jnp.bfloat16)
-    d_up = (d_hidden * act).astype(jnp.bfloat16)
-    d_gate = (d_hidden * up * s * (1.0 + gate * (1.0 - s))).astype(jnp.bfloat16)
-    return hidden, d_gate, d_up
-
-
-def weight_grad(acts, x, dy):
-    hidden, d_gate, d_up = acts
-    dot = functools.partial(jnp.dot, preferred_element_type=jnp.float32)
-    return jnp.concatenate([dot(d_gate, x), dot(d_up, x), dot(hidden, dy)], axis=1)
+def expert_kernel(
+    peers, groups, own_ref, mate_ref, w_ref, back_ref, g_ref,
+    rows, weights, acts, turned, grad_in, partial, theirs,
+    row_sem, w_sem, bar_send, bar_recv, dx_send, dx_recv, keep_sem,
+):
+    e = lax.axis_index("expert")
+    r = lax.axis_index("replica")
+    step = step_of(e, r)
+    other = lax.rem(r + groups - step, groups)
+    held, width = own_ref.shape[1], own_ref.shape[2]
+    hidden = w_ref.shape[0]
+    shard = hidden // groups
+    chunk = partial.shape[2]
+    chunks = partial.shape[0]
+    per = width // chunk
+    cap = held // peers
+    f32, bf16 = jnp.float32, jnp.bfloat16
+
+    barrier = pltpu.get_barrier_semaphore()
+    for k in range(1, peers):
+        pl.semaphore_signal(barrier, inc=1, device_id=((e + k) % peers, r), device_id_type=MESH)
+    pl.semaphore_signal(barrier, inc=1, device_id=(e, other), device_id_type=MESH)
+
+    shards = [other, r, lax.rem(r + groups + step, groups), lax.rem(r + 2, groups)]
+    loads = [
+        pltpu.make_async_copy(
+            w_ref.at[pl.ds(pl.multiple_of(at * shard, 32), shard), :],
+            weights.at[pl.ds(i * shard, shard), :],
+            w_sem.at[i],
+        )
+        for i, at in enumerate(shards)
+    ]
+    takes = [
+        pltpu.make_async_copy(ref.at[a], rows.at[a, pl.ds(p * held, held), :], row_sem.at[a, p])
+        for a in (0, 1)
+        for p, ref in enumerate((own_ref, mate_ref))
+    ]
+    for copy in loads[:1] + takes + loads[1:]:
+        copy.start()
+
+    def forward(i, first, count):
+        span = 256
+        ws = pl.ds(i * shard, shard)
+
+        def tile(t, _):
+            at = pl.ds(pl.multiple_of(first + t * span, span), span)
+            dims = (((1,), (1,)), ((), ()))
+            gate = lax.dot_general(weights[ws, 0:width], rows[0, at, :], dims, preferred_element_type=f32)
+            up = lax.dot_general(weights[ws, width : 2 * width], rows[0, at, :], dims, preferred_element_type=f32)
+            d_hidden = lax.dot_general(
+                weights[ws, 2 * width : 3 * width], rows[1, at, :], dims, preferred_element_type=f32
+            )
+            s = jax.nn.sigmoid(gate)
+            act = gate * s
+            acts[0, ws, at] = (d_hidden * up * s * (1.0 + gate * (1.0 - s))).astype(bf16)
+            acts[1, ws, at] = (d_hidden * act).astype(bf16)
+            acts[2, ws, at] = (act * up).astype(bf16)
+            return 0
+
+        lax.fori_loop(0, count // span, tile, 0)
+
+    def weight_grad(i, j):
+        part = j // per
+        cols = pl.ds(pl.multiple_of(lax.rem(j, per) * chunk, chunk), chunk)
+        return jnp.dot(
+            acts[part, pl.ds(i * shard, shard), :], rows[part // 2, :, cols], preferred_element_type=f32
+        )
+
+    def send_partial(j):
+        return pltpu.make_async_remote_copy(
+            src_ref=partial.at[j], dst_ref=theirs.at[j], send_sem=bar_send.at[j], recv_sem=bar_recv.at[j],
+            device_id=(e, other), device_id_type=MESH,
+        )
+
+    z, x, c = e // 8, (e // 2) % 4, e % 2
+    order = [
+        ((z + dz) % 4) * 8 + ((x + dx) % 4) * 2 + (c + dc) % 2
+        for dz, dx in OFFSETS
+        for dc in (0, 1)
+        if (dz, dx, dc) != (0, 0, 0)
+    ]
+    halves = 2
+    half = width // halves
+
+    def send_rows(h, to):
+        cols = pl.ds(h * half, half)
+        return pltpu.make_async_remote_copy(
+            src_ref=grad_in.at[to, :, cols], dst_ref=back_ref.at[e, :, cols], send_sem=dx_send.at[h],
+            recv_sem=dx_recv.at[h], device_id=(to, r), device_id_type=MESH,
+        )
+
+    def all_rows(h):
+        cols = pl.ds(h * half, half)
+        some = pl.ds(0, peers - 1)
+        return pltpu.make_async_remote_copy(
+            src_ref=grad_in.at[some, :, cols], dst_ref=back_ref.at[some, :, cols], send_sem=dx_send.at[h],
+            recv_sem=dx_recv.at[h], device_id=(e, other), device_id_type=MESH,
+        )
+
+    def keep(h):
+        cols = pl.ds(h * half, half)
+        return pltpu.make_async_copy(grad_in.at[e, :, cols], back_ref.at[e, :, cols], keep_sem.at[h])
+
+    for copy in loads[:1] + takes:
+        copy.wait()
+    forward(0, 0, 2 * held)
+    pl.semaphore_wait(barrier, peers)
+
+    def first_pass(j, _):
+        partial[j] = weight_grad(0, j).astype(bf16)
+
+        @pl.when(j > 0)
+        def _():
+            send_partial(j - 1).start()
+
+        return 0
+
+    lax.fori_loop(0, chunks, first_pass, 0)
+    for copy in loads[1:]:
+        copy.wait()
+    send_partial(chunks - 1).start()
+    for i in range(1, groups):
+        forward(i, 0, held)
+
+    def turn(t, _):
+        at = pl.ds(pl.multiple_of(t * 128, 128), 128)
+        for part in (0, 1):
+            turned[part, at, :] = jnp.transpose(acts[part, :, at])
+        return 0
+
+    lax.fori_loop(0, held // 128, turn, 0)
+
+    for h in range(halves):
+
+        def columns(t, _):
+            at = pl.multiple_of(h * half + t * chunk, chunk)
+            total = jnp.dot(turned[0], weights[:, pl.ds(at, chunk)], preferred_element_type=f32)
+            total += jnp.dot(turned[1], weights[:, pl.ds(width + at, chunk)], preferred_element_type=f32)
+            grad_in[:, :, pl.ds(at, chunk)] = total.astype(bf16).reshape(peers, cap, chunk)
+            return 0
+
+        lax.fori_loop(0, half // chunk, columns, 0)
+        for to in order:
+            send_rows(h, to).start()
+        keep(h).start()
+
+    forward(1, held, held)
+
+    def second_pass(j, _):
+        mine = weight_grad(1, j)
+        send_partial(j).wait_recv()
+        g_ref[:, pl.ds(pl.multiple_of(j * chunk, chunk), chunk)] = (mine + theirs[j].astype(f32)).astype(bf16)
+        return 0
+
+    lax.fori_loop(0, chunks, second_pass, 0)
+    for h in range(halves):
+        all_rows(h).wait()
+        keep(h).wait()
+
+    def drain(j, _):
+        send_partial(j).wait_send()
+        return 0
+
+    lax.fori_loop(0, chunks, drain, 0)
+
+
+def expert_backward(own, mate, weights, peers, groups):
+    held, width = own.shape[1:]
+    hidden = weights.shape[0]
+    shard, chunk = hidden // groups, 512
+    chunks = 3 * width // chunk
+    anywhere = pl.BlockSpec(memory_space=pl.ANY)
+    bf16 = own.dtype
+    return pl.pallas_call(
+        functools.partial(expert_kernel, peers, groups),
+        out_shape=(
+            jax.ShapeDtypeStruct((peers, held // peers, width), bf16),
+            jax.ShapeDtypeStruct((shard, 3 * width), bf16),
+        ),
+        in_specs=[anywhere] * 3,
+        out_specs=(anywhere, pl.BlockSpec(memory_space=pltpu.VMEM)),
+        scratch_shapes=[
+            pltpu.VMEM((2, 2 * held, width), bf16),
+            pltpu.VMEM((hidden, 3 * width), bf16),
+            pltpu.VMEM((3, hidden, 2 * held), bf16),
+            pltpu.VMEM((2, held, hidden), bf16),
+            pltpu.VMEM((peers, held // peers, width), bf16),
+            pltpu.VMEM((chunks, shard, chunk), bf16),
+            pltpu.VMEM((chunks, shard, chunk), bf16),
+            pltpu.SemaphoreType.DMA((2, 2)),
+            pltpu.SemaphoreType.DMA((groups,)),
+            pltpu.SemaphoreType.DMA((chunks,)),
+            pltpu.SemaphoreType.DMA((chunks,)),
+            pltpu.SemaphoreType.DMA((2,)),
+            pltpu.SemaphoreType.DMA((2,)),
+            pltpu.SemaphoreType.DMA((2,)),
+        ],
+        compiler_params=pltpu.CompilerParams(
+            collective_id=1, has_side_effects=True, vmem_limit_bytes=62 * 1024 * 1024
+        ),
+        name="expert_backward",
+    )(own, mate, weights)
 
 
 def body(x_tokens, d_out, expert_ids, combine, w_stack):
@@ -118,8 +300,6 @@
     experts, groups = lax.axis_size("expert"), lax.axis_size("replica")
     capacity = 2 * tokens * expert_ids.shape[1] // experts
     slots = experts * capacity
-    e, r = lax.axis_index("expert"), lax.axis_index("replica")
-    other = (r + groups - step_of(e, r)) % groups
 
     ids = expert_ids.T
     iota = jnp.arange(experts, dtype=jnp.int32)
@@ -139,43 +319,11 @@
 
     own, mate = dispatch(send, groups)
     own, mate = own.reshape(2, slots, width), mate.reshape(2, slots, width)
-    weights = w_stack[0]
-    hidden = weights.shape[0]
-    shard = hidden // groups
-
-    w_other = lax.dynamic_slice_in_dim(weights, other * shard, shard, 0)
-    w_mine = lax.dynamic_slice_in_dim(weights, r * shard, shard, 0)
-
-    def both_planes(w):
-        a, b = forward(w, own[0], own[1], width), forward(w, mate[0], mate[1], width)
-        ga, gb = weight_grad(a, own[0], own[1]), weight_grad(b, mate[0], mate[1])
-        return ga + gb
-
-    pairs = []
-    for i in range(experts):
-        for g in range(groups):
-            pairs.append((i * groups + g, i * groups + (g - step_of(i, g)) % groups))
-    partial = both_planes(w_other).astype(jnp.bfloat16)
-    theirs = lax.ppermute(partial, ("expert", "replica"), pairs)
-    own, mate, partial = lax.optimization_barrier((own, mate, partial))
-
-    _, d_gate, d_up = forward(weights, own[0], own[1], width)
-    rows = (((0,), (0,)), ((), ()))
-    dx = lax.dot_general(d_gate, weights[:, :width], rows, preferred_element_type=jnp.float32) + lax.dot_general(
-        d_up, weights[:, width : 2 * width], rows, preferred_element_type=jnp.float32
-    )
-    dx = dx.astype(jnp.bfloat16)
-    own, mate, dx = lax.optimization_barrier((own, mate, dx))
-    back = lax.all_to_all(
-        dx.reshape(experts, capacity, width), "expert", split_axis=0, concat_axis=0, tiled=True
-    )
+    back, g_shard = expert_backward(own, mate, w_stack[0], experts, groups)
     d_tokens = lax.dot_general(
-        place, back.reshape(slots, width), rows, preferred_element_type=jnp.float32
+        place, back.reshape(slots, width), (((0,), (0,)), ((), ())), preferred_element_type=jnp.float32
     ).astype(jnp.bfloat16)
-
-    mine = both_planes(w_mine)
-    g_stack = (mine + theirs.astype(jnp.float32)).astype(jnp.bfloat16)
-    return d_tokens, g_stack[None]
+    return d_tokens, g_shard[None]
 
 
 def solution(mesh):

time: 206 us -> 147 us (0.71); the launches traced: 202 us -> 147 us
  matrix products: 91.1 us -> 5.48 us
  Pallas kernels: 63.1 us -> 129 us
  other arithmetic: 18.2 us -> 1.38 us
  local copies, waits for them, and re-layouts: 17.8 us -> 10.3 us
  starting transfers between devices: 7.48 us -> 0 us
  waiting for transfers between devices: 3.11 us -> 0 us
    dot_general x29 -> x1, matrix products: 89.5 us -> 2.88 us  [body(): lax.dot_general(place, back.reshape(slots, width), (((0,), (0,)), ((), ()...]
    pallas_call x0 -> x1, Pallas kernels: none -> 65.8 us  [expert_backward(): pl.pallas_call(functools.partial(expert_kernel, peers, groups), out_shape...]
    broadcast_in_dim x1 -> x0, other arithmetic: 10.2 us -> none  [body(): return (d_tokens, g_stack[None])]
    dynamic_slice x1 -> x0, local copies, waits for them, and re-layouts: 7.41 us -> none  [body(): w_mine = lax.dynamic_slice_in_dim(weights, r * shard, shard, 0)]
    convert_element_type x1 -> x0, other arithmetic: 6.6 us -> none  [body(): partial = both_planes(w_other).astype(jnp.bfloat16)]
    all_to_all x1 -> x0, starting transfers between devices: 5.14 us -> none  [body(): lax.all_to_all(dx.reshape(experts, capacity, width), 'expert', split_axis...]
    all_to_all x1 -> x0, waiting for transfers between devices: 3.11 us -> none  [body(): lax.all_to_all(dx.reshape(experts, capacity, width), 'expert', split_axis...]
    ppermute x1 -> x0, starting transfers between devices: 2.34 us -> none  [body(): theirs = lax.ppermute(partial, ('expert', 'replica'), pairs)]
  transfers between devices with their start and end apart: 2 -> 0, of which waited for: 1 -> 0; matrix products, arithmetic and copies ran while one was open for 34% -> 0% of each run, Pallas kernels for 0% -> 0%
where the time goes in v2:
time: 147 us
  Pallas kernels  129 us (88%)
  local copies, waits for them, and re-layouts  10.3 us (7%)
  matrix products  5.48 us (4%)
    pallas_call x1, Pallas kernels, expert_backward(): pl.pallas_call(functools.partial(expert_kernel, peers, groups), out_shape...  65.8 us
    pallas_call x1, Pallas kernels, dispatch(): pl.pallas_call(functools.partial(dispatch_kernel, send.shape[1], groups),...  63.2 us
    unnamed x7, local copies, waits for them, and re-layouts  8.76 us

profile of v2, /device:TPU:0, one launch (start us, length us, event | category | flops | bytes accessed | tf_op | source)
XLA Modules:
  0.0 146.8 jit_solution(1451536261891238717)
XLA Ops:
  0.6 0.0 copy-start
  0.6 0.8 slice_bitcast_fusion.3
  1.4 0.2 select_reduce_fusion.2
  1.6 0.8 fusion.16
  2.3 0.8 slice_bitcast_fusion
  3.1 0.2 select_reduce_fusion
  3.3 0.0 copy-done
  3.3 0.7 multiply_convert_fusion
  4.0 1.7 %convolution_convert_fusion = bf16[512,2048]{1,0:T(8,128)(2,1)S(1)} fusion(bf16[128,2048]{1,0:T(8,128)(2,1)} %param.5, s32[128]{0:T(128)S(1)} %get-tuple-element.12, s32[128]{0:T(128)S(1)} %get-tuple-element.13), kind=kOutput, calls=%fused_computation.2 | convolution fusion | flops 269680640 | bytes 2622464 | tf_op jit(solution)/shard_map/dot_general | solution.py:316
  5.8 0.4 pad_maximum_fusion.send_ref
  6.2 63.2 %dispatch.1 = (bf16[2,32,16,2048]{3,2,1,0:T(8,128)(2,1)S(1)}, bf16[2,32,16,2048]{3,2,1,0:T(8,128)(2,1)S(1)}) custom-call(bf16[2,32,16,2048]{3,2,1,0:T(8,128)(2,1)S(1)} %pad_maximum_fusion.send_ref), custom_call_target="tpu_custom_call" | custom-call | tf_op jit(solution)/shard_map/dispatch/pallas_call | solution.py:81
  69.4 0.0 copy-start.1
  69.4 2.0 %copy-done.1 = bf16[2,32,16,2048]{3,2,1,0:T(8,128)(2,1)} copy-done((bf16[2,32,16,2048]{3,2,1,0:T(8,128)(2,1)}, bf16[2,32,16,2048]{3,2,1,0:T(8,128)(2,1)S(1)}, u32[]{:S(2)}) %copy-start.1) | copy-done | bytes 4194328
  71.4 0.0 copy-start.2
  71.4 2.0 %copy-done.2 = bf16[2,32,16,2048]{3,2,1,0:T(8,128)(2,1)} copy-done((bf16[2,32,16,2048]{3,2,1,0:T(8,128)(2,1)}, bf16[2,32,16,2048]{3,2,1,0:T(8,128)(2,1)S(1)}, u32[]{:S(2)}) %copy-start.2) | copy-done | bytes 4194328
  73.4 65.8 %expert_backward.1 = (bf16[32,16,2048]{2,1,0:T(8,128)(2,1)}, bf16[352,6144]{1,0:T(8,128)(2,1)}) custom-call(bf16[2,512,2048]{2,1,0:T(8,128)(2,1)} %bitcast.31, bf16[2,512,2048]{2,1,0:T(8,128)(2,1)} %bitcast.32, bf16[1408,6144]{1,0:T(8,128)(2,1)} %bitcast.33), custom_call_target="tpu_custom_call" | custom-call | tf_op jit(solution)/shard_map/expert_backward/pallas_call | solution.py:267
  139.2 2.9 %convolution_convert_fusion.1 = bf16[128,2048]{1,0:T(8,128)(2,1)} fusion(bf16[512,2048]{1,0:T(8,128)(2,1)} %bitcast.37, s32[128]{0:T(128)S(1)} %get-tuple-element.12, s32[128]{0:T(128)S(1)} %get-tuple-element.13), kind=kOutput, calls=%fused_computation.3 | convolution fusion | flops 268894208 | bytes 2622464 | tf_op jit(solution)/shard_map/dot_general | solution.py:323
  142.1 4.8 %copy.8 = bf16[1,352,6144]{2,1,0:T(8,128)(2,1)} copy(bf16[1,352,6144]{2,1,0:T(8,128)(2,1)} %bitcast.36) | data formatting | bytes 8650752
  (1 shorter events, 0.0 us)
Async XLA Ops:
  0.6 2.7 %copy-start = (bf16[128,2048]{1,0:T(8,128)(2,1)S(1)}, bf16[128,2048]{1,0:T(8,128)(2,1)}, u32[]{:S(2)}) copy-start(bf16[128,2048]{1,0:T(8,128)(2,1)} %param.6) | copy-start | bytes 1572868
  69.4 2.0 %copy-start.1 = (bf16[2,32,16,2048]{3,2,1,0:T(8,128)(2,1)}, bf16[2,32,16,2048]{3,2,1,0:T(8,128)(2,1)S(1)}, u32[]{:S(2)}) copy-start(bf16[2,32,16,2048]{3,2,1,0:T(8,128)(2,1)S(1)} %get-tuple-element.6) | copy-start | bytes 12582916
  71.4 2.0 %copy-start.2 = (bf16[2,32,16,2048]{3,2,1,0:T(8,128)(2,1)}, bf16[2,32,16,2048]{3,2,1,0:T(8,128)(2,1)S(1)}, u32[]{:S(2)}) copy-start(bf16[2,32,16,2048]{3,2,1,0:T(8,128)(2,1)S(1)} %get-tuple-element.7) | copy-start | bytes 12582916
